TPU v7x, 512 devices: a whole 4x8x8 slice. The times are simulated.
512 devices in a mesh: ctx: 64 (over y, x, core), tp: 8 (over z).
Axes of the slice: x: 4, y: 8, z: 8, core: 2. Of those that a mesh axis runs over, the one named last changes fastest.
Arguments:
- queries: bfloat16 [16384, 8192], P('ctx', 'tp'), may hold values from -6 to 6
- key_branch: bfloat16 [16384, 8192], P('ctx', 'tp'), may hold values from -6 to 6
- value_branch: bfloat16 [16384, 8192], P('ctx', 'tp'), may hold values from -6 to 6
- cotangent: bfloat16 [16384, 8192], P('ctx', 'tp'), may hold values from -6 to 6
- filters: float32 [512, 128], replicated, may hold values from -0.5 to 0.5
- skip_bias: float32 [8192], P('tp'), may hold values from -1 to 1
- contig_start: int32 [16384], replicated, may hold values from 0 to 16383, as said below
Outputs:
- output: bfloat16 [16384, 8192], P('ctx', 'tp')
- grad_query: bfloat16 [16384, 8192], P('ctx', 'tp')
- grad_key: bfloat16 [16384, 8192], P('ctx', 'tp')
- grad_value: bfloat16 [16384, 8192], P('ctx', 'tp')
- grad_filter: float32 [512, 128], replicated
- grad_bias: float32 [8192], P('tp')
Inputs may be any that keep to these rules, and one draw needn't show every extreme that they name: contig_start[0] is 0, and for t > 0 contig_start[t] is either t (a new contig begins) or contig_start[t - 1]; the last token begins a contig of its own.
All inputs are finite; a program needn't handle non-finite values.
Results may differ from a plain program's by a relative error of at most 0.0056.
Values may be sent and summed in bfloat16 or wider, within the bound.
A program may use at most 64 MiB of HBM per device.

v0:
```python
import math
import jax
import jax.numpy as jnp
from jax import lax
from jax.sharding import PartitionSpec as P


def toeplitz(filter_taps):
    group_count, filter_size = filter_taps.shape
    leading = jnp.zeros((group_count, 1), filter_taps.dtype)
    trailing = jnp.zeros((group_count, filter_size), filter_taps.dtype)
    pattern = jnp.concatenate([leading, filter_taps[:, ::-1], trailing], axis=1)
    tiled = jnp.tile(pattern, (1, filter_size))[:, : 2 * filter_size * filter_size]
    return tiled.reshape(group_count, filter_size, 2 * filter_size)


def fold_lags(products):
    group_count, filter_size, window_size = products.shape
    flattened = products.reshape(group_count, filter_size * window_size)
    flattened = jnp.concatenate(
        [flattened, jnp.zeros((group_count, filter_size), products.dtype)], axis=1
    )
    columns = flattened.reshape(group_count, filter_size, window_size + 1).sum(axis=1)
    return columns[:, 1 : filter_size + 1][:, ::-1]


def hyena_pass(
    queries,
    key_branch,
    value_branch,
    cotangent,
    gated_signal,
    signal_grad,
    left_rim,
    right_rim,
    row_starts,
    next_starts,
    filter_taps,
    bias_part,
    first_row,
):
    row_count, channel_count = gated_signal.shape
    group_count, filter_size = filter_taps.shape
    per_group = channel_count // group_count
    block_count = row_count // filter_size
    padded = jnp.concatenate(
        [jnp.zeros((1, channel_count), jnp.bfloat16), left_rim, gated_signal], axis=0
    )
    windows = jnp.concatenate(
        [
            padded[:row_count].reshape(block_count, filter_size, group_count, per_group),
            padded[filter_size:].reshape(block_count, filter_size, group_count, per_group),
        ],
        axis=1,
    )
    grads_ext = jnp.concatenate(
        [signal_grad, right_rim, jnp.zeros((1, channel_count), jnp.bfloat16)], axis=0
    )
    grads_ext = grads_ext.reshape(block_count + 1, filter_size, group_count, per_group)
    starts_ext = jnp.concatenate([row_starts, next_starts]).reshape(block_count + 1, filter_size)
    source_pos = (
        first_row + (jnp.arange(block_count + 1, dtype=jnp.int32)[:, None] - 1) * filter_size
    )
    source_pos = source_pos + jnp.arange(2 * filter_size, dtype=jnp.int32)[None, :]
    visible = source_pos[:, None, :] >= starts_ext[:, :, None]
    band = jnp.where(visible[:, None], toeplitz(filter_taps)[None], jnp.zeros((), jnp.bfloat16))
    convolved = jnp.einsum(
        "bgts,bsgc->btgc", band[:block_count], windows, preferred_element_type=jnp.float32
    ).reshape(row_count, channel_count)
    back_terms = jnp.einsum("bgts,btgc->bsgc", band, grads_ext, preferred_element_type=jnp.float32)
    gated_grad = (back_terms[:block_count, filter_size:] + back_terms[1:, :filter_size]).reshape(
        row_count, channel_count
    )
    filtered = convolved + bias_part[None, :] * gated_signal.astype(jnp.float32)
    output = (queries.astype(jnp.float32) * filtered).astype(jnp.bfloat16)
    grad_query = (cotangent.astype(jnp.float32) * filtered).astype(jnp.bfloat16)
    gated_grad = gated_grad + bias_part[None, :] * signal_grad.astype(jnp.float32)
    grad_key = (gated_grad * value_branch.astype(jnp.float32)).astype(jnp.bfloat16)
    grad_value = (gated_grad * key_branch.astype(jnp.float32)).astype(jnp.bfloat16)
    bias_term = jnp.sum(signal_grad.astype(jnp.float32) * gated_signal.astype(jnp.float32), axis=0)
    products = jnp.einsum(
        "btgc,bsgc->bgts", grads_ext[:block_count], windows, preferred_element_type=jnp.float32
    )
    products = jnp.where(visible[:block_count, None], products, jnp.zeros((), jnp.float32)).sum(
        axis=0
    )
    return (output, grad_query, grad_key, grad_value, fold_lags(products), bias_term)


def gate_pair(first_input, second_input):
    return (first_input.astype(jnp.float32) * second_input.astype(jnp.float32)).astype(jnp.bfloat16)


def body(queries, key_branch, value_branch, cotangent, filters, skip_bias, contig_start):
    row_count, channel_count = queries.shape
    group_total, filter_size = filters.shape
    ctx_count = lax.axis_size("ctx")
    tp_count = lax.axis_size("tp")
    shard_index = lax.axis_index("ctx")
    tensor_index = lax.axis_index("tp")
    token_count = row_count * ctx_count
    per_group = channel_count * tp_count // group_total
    starts_pad = jnp.concatenate([contig_start, jnp.zeros((filter_size,), jnp.int32)])
    moved = (
        lax.all_to_all(queries, "ctx", split_axis=1, concat_axis=0, tiled=True),
        lax.all_to_all(key_branch, "ctx", split_axis=1, concat_axis=0, tiled=True),
        lax.all_to_all(value_branch, "ctx", split_axis=1, concat_axis=0, tiled=True),
        lax.all_to_all(cotangent, "ctx", split_axis=1, concat_axis=0, tiled=True),
    )
    query_full, key_full, value_full, cotangent_full = moved
    column_count = channel_count // ctx_count
    held_groups = max(1, column_count // per_group)
    gated_signal = gate_pair(key_full, value_full)
    signal_grad = gate_pair(cotangent_full, query_full)
    group_first = (tensor_index * channel_count + shard_index * column_count) // per_group
    filter_taps = lax.dynamic_slice_in_dim(filters, group_first, held_groups, 0).astype(
        jnp.bfloat16
    )
    bias_slice = lax.dynamic_slice_in_dim(skip_bias, shard_index * column_count, column_count, 0)
    slab_rows = 8 * filter_size
    slab_count = token_count // slab_rows
    signal_pad = jnp.concatenate(
        [jnp.zeros((filter_size - 1, column_count), jnp.bfloat16), gated_signal], axis=0
    )
    grad_pad = jnp.concatenate(
        [signal_grad, jnp.zeros((filter_size - 1, column_count), jnp.bfloat16)], axis=0
    )

    def one_slab(slab_index):
        first_row = slab_index * slab_rows

        def rows_of(array):
            return lax.dynamic_slice_in_dim(array, first_row, slab_rows, 0)

        return hyena_pass(
            rows_of(query_full),
            rows_of(key_full),
            rows_of(value_full),
            rows_of(cotangent_full),
            rows_of(gated_signal),
            rows_of(signal_grad),
            lax.dynamic_slice_in_dim(signal_pad, first_row, filter_size - 1, 0),
            lax.dynamic_slice_in_dim(grad_pad, first_row + slab_rows, filter_size - 1, 0),
            lax.dynamic_slice_in_dim(contig_start, first_row, slab_rows, 0),
            lax.dynamic_slice_in_dim(starts_pad, first_row + slab_rows, filter_size, 0),
            filter_taps,
            bias_slice,
            first_row,
        )

    pieces = lax.map(one_slab, jnp.arange(slab_count, dtype=jnp.int32))
    results = tuple((piece.reshape(token_count, column_count) for piece in pieces[:4]))
    returned = (
        lax.all_to_all(results[0], "ctx", split_axis=0, concat_axis=1, tiled=True),
        lax.all_to_all(results[1], "ctx", split_axis=0, concat_axis=1, tiled=True),
        lax.all_to_all(results[2], "ctx", split_axis=0, concat_axis=1, tiled=True),
        lax.all_to_all(results[3], "ctx", split_axis=0, concat_axis=1, tiled=True),
    )
    output, grad_query, grad_key, grad_value = returned
    filter_part = lax.dynamic_update_slice(
        jnp.zeros((group_total, filter_size), jnp.float32), pieces[4].sum(axis=0), (group_first, 0)
    )
    bias_part = lax.dynamic_update_slice(
        jnp.zeros((channel_count,), jnp.float32),
        pieces[5].sum(axis=0),
        (shard_index * column_count,),
    )
    filter_sum = lax.psum(filter_part, ("ctx", "tp"))
    bias_sum = lax.psum(bias_part, "ctx")
    grad_filter = filter_sum * (1.0 / math.sqrt(token_count * per_group))
    grad_bias = bias_sum * (1.0 / math.sqrt(token_count))
    return (output, grad_query, grad_key, grad_value, grad_filter, grad_bias)


def solution(mesh):
    return jax.shard_map(
        body,
        mesh=mesh,
        in_specs=(
            P("ctx", "tp"),
            P("ctx", "tp"),
            P("ctx", "tp"),
            P("ctx", "tp"),
            P(),
            P("tp"),
            P(),
        ),
        out_specs=(P("ctx", "tp"), P("ctx", "tp"), P("ctx", "tp"), P("ctx", "tp"), P(), P("tp")),
        check_vma=False,
    )
```

profile of v0, /device:TPU:23, one launch (start us, length us, event | category | flops | bytes accessed | tf_op | source)
XLA Modules:
  0.0 609.2 jit_solution(8776793197152598005)
XLA Ops:
  7.2 2.1 copy.73
  9.3 10.8 %all-to-all-start.1 = ((bf16[256,64,16]{0,2,1:T(8,128)(2,1)}), bf16[256,64,16]{0,2,1:T(8,128)(2,1)S(1)}, u32[]{:S(2)}, u32[]{:S(2)}) async-start(bf16[256,64,16]{0,2,1:T(8,128)(2,1)} %bitcast.17), calls=%async_computation.1 | async-start | bytes 1048576 | tf_op jit(solution)/shard_map/all_to_all | solution.py:106
  20.1 1.0 copy.75
  21.1 14.1 %all-to-all-done.1 = bf16[256,64,16]{0,2,1:T(8,128)(2,1)S(1)} async-done(((bf16[256,64,16]{0,2,1:T(8,128)(2,1)}), bf16[256,64,16]{0,2,1:T(8,128)(2,1)S(1)}, u32[]{:S(2)}, u32[]{:S(2)}) %all-to-all-start.1) | async-done | bytes 524320 | tf_op jit(solution)/shard_map/all_to_all | solution.py:106
  35.2 8.3 %all-to-all-start.2 = ((bf16[256,64,16]{0,2,1:T(8,128)(2,1)}), bf16[256,64,16]{0,2,1:T(8,128)(2,1)S(1)}, u32[]{:S(2)}, u32[]{:S(2)}) async-start(bf16[256,64,16]{0,2,1:T(8,128)(2,1)} %bitcast.19), calls=%async_computation.2 | async-start | bytes 1048576 | tf_op jit(solution)/shard_map/all_to_all | solution.py:107
  43.5 1.0 copy.71
  44.5 14.1 %all-to-all-done.2 = bf16[256,64,16]{0,2,1:T(8,128)(2,1)S(1)} async-done(((bf16[256,64,16]{0,2,1:T(8,128)(2,1)}), bf16[256,64,16]{0,2,1:T(8,128)(2,1)S(1)}, u32[]{:S(2)}, u32[]{:S(2)}) %all-to-all-start.2) | async-done | bytes 524320 | tf_op jit(solution)/shard_map/all_to_all | solution.py:107
  58.6 8.3 %all-to-all-start = ((bf16[256,64,16]{0,2,1:T(8,128)(2,1)}), bf16[256,64,16]{0,2,1:T(8,128)(2,1)S(1)}, u32[]{:S(2)}, u32[]{:S(2)}) async-start(bf16[256,64,16]{0,2,1:T(8,128)(2,1)} %bitcast.15), calls=%async_computation | async-start | bytes 1048576 | tf_op jit(solution)/shard_map/all_to_all | solution.py:105
  66.9 1.0 copy.77
  67.9 14.1 %all-to-all-done = bf16[256,64,16]{0,2,1:T(8,128)(2,1)S(1)} async-done(((bf16[256,64,16]{0,2,1:T(8,128)(2,1)}), bf16[256,64,16]{0,2,1:T(8,128)(2,1)S(1)}, u32[]{:S(2)}, u32[]{:S(2)}) %all-to-all-start) | async-done | bytes 524320 | tf_op jit(solution)/shard_map/all_to_all | solution.py:105
  82.0 8.4 %all-to-all-start.3 = ((bf16[256,64,16]{0,2,1:T(8,128)(2,1)}), bf16[256,64,16]{0,2,1:T(8,128)(2,1)S(1)}, u32[]{:S(2)}, u32[]{:S(2)}) async-start(bf16[256,64,16]{0,2,1:T(8,128)(2,1)} %bitcast.21), calls=%async_computation.3 | async-start | bytes 1048576 | tf_op jit(solution)/shard_map/all_to_all | solution.py:108
  91.4 14.1 %all-to-all-done.3 = bf16[256,64,16]{0,2,1:T(8,128)(2,1)S(1)} async-done(((bf16[256,64,16]{0,2,1:T(8,128)(2,1)}), bf16[256,64,16]{0,2,1:T(8,128)(2,1)S(1)}, u32[]{:S(2)}, u32[]{:S(2)}) %all-to-all-start.3) | async-done | bytes 524320 | tf_op jit(solution)/shard_map/all_to_all | solution.py:108
  105.7 1.0 concatenate.42
  106.7 0.9 multiply_convert_fusion.4
  107.6 1.9 concatenate.44
  109.5 122.1 %while.22 = (s32[]{:T(128)}, bf16[16,1024,16]{1,2,0:T(8,128)(2,1)}, bf16[16,1024,16]{1,2,0:T(8,128)(2,1)}, bf16[16,1024,16]{1,2,0:T(8,128)(2,1)}, bf16[16,1024,1...) while((s32[]{:T(128)}, bf16[16,1024,16]{1,2,0:T(8,128)(2,1)}, ...), condition=%wide.region_4.5_spmd, body=%wide.region_0.4_spmd.sunk | while | flops 28791580 | bytes 4254939 | solution.py:151
  111.5 0.9 fusion.48
  119.2 0.9 fusion.48
  126.8 0.9 fusion.48
  134.4 0.9 fusion.48
  142.0 0.9 fusion.48
  149.7 0.9 fusion.48
  157.3 0.9 fusion.48
  164.9 0.9 fusion.48
  172.6 0.9 fusion.48
  195.5 0.9 fusion.48
  203.1 0.9 fusion.48
  218.4 0.9 fusion.48
  226.0 0.9 fusion.48
  231.6 1.3 copy.79
  233.3 1.1 copy.80
  234.3 8.4 %all-to-all-start.4 = ((bf16[64,256,16]{1,2,0:T(8,128)(2,1)}), bf16[64,256,16]{1,2,0:T(8,128)(2,1)S(1)}, u32[]{:S(2)}, u32[]{:S(2)}) async-start(bf16[64,256,16]{1,2,0:T(8,128)(2,1)} %copy.80), calls=%async_computation.4 | async-start | bytes 1048576 | tf_op jit(solution)/shard_map/all_to_all | solution.py:154
  243.4 1.1 copy.82
  244.5 13.4 %all-to-all-done.4 = bf16[64,256,16]{1,2,0:T(8,128)(2,1)S(1)} async-done(((bf16[64,256,16]{1,2,0:T(8,128)(2,1)}), bf16[64,256,16]{1,2,0:T(8,128)(2,1)S(1)}, u32[]{:S(2)}, u32[]{:S(2)}) %all-to-all-start.4) | async-done | bytes 524320 | tf_op jit(solution)/shard_map/all_to_all | solution.py:154
  257.9 8.5 %all-to-all-start.5 = ((bf16[64,256,16]{1,2,0:T(8,128)(2,1)}), bf16[64,256,16]{1,2,0:T(8,128)(2,1)S(1)}, u32[]{:S(2)}, u32[]{:S(2)}) async-start(bf16[64,256,16]{1,2,0:T(8,128)(2,1)} %copy.82), calls=%async_computation.5 | async-start | bytes 1048576 | tf_op jit(solution)/shard_map/all_to_all | solution.py:155
  267.0 1.1 copy.84
  268.1 13.4 %all-to-all-done.5 = bf16[64,256,16]{1,2,0:T(8,128)(2,1)S(1)} async-done(((bf16[64,256,16]{1,2,0:T(8,128)(2,1)}), bf16[64,256,16]{1,2,0:T(8,128)(2,1)S(1)}, u32[]{:S(2)}, u32[]{:S(2)}) %all-to-all-start.5) | async-done | bytes 524320 | tf_op jit(solution)/shard_map/all_to_all | solution.py:155
  281.4 8.3 %all-to-all-start.6 = ((bf16[64,256,16]{1,2,0:T(8,128)(2,1)}), bf16[64,256,16]{1,2,0:T(8,128)(2,1)S(1)}, u32[]{:S(2)}, u32[]{:S(2)}) async-start(bf16[64,256,16]{1,2,0:T(8,128)(2,1)} %copy.84), calls=%async_computation.6 | async-start | bytes 1048576 | tf_op jit(solution)/shard_map/all_to_all | solution.py:156
  290.4 1.1 copy.86
  291.4 13.4 %all-to-all-done.6 = bf16[64,256,16]{1,2,0:T(8,128)(2,1)S(1)} async-done(((bf16[64,256,16]{1,2,0:T(8,128)(2,1)}), bf16[64,256,16]{1,2,0:T(8,128)(2,1)S(1)}, u32[]{:S(2)}, u32[]{:S(2)}) %all-to-all-start.6) | async-done | bytes 524320 | tf_op jit(solution)/shard_map/all_to_all | solution.py:156
  304.8 8.3 %all-to-all-start.7 = ((bf16[64,256,16]{1,2,0:T(8,128)(2,1)}), bf16[64,256,16]{1,2,0:T(8,128)(2,1)S(1)}, u32[]{:S(2)}, u32[]{:S(2)}) async-start(bf16[64,256,16]{1,2,0:T(8,128)(2,1)} %copy.86), calls=%async_computation.7 | async-start | bytes 1048576 | tf_op jit(solution)/shard_map/all_to_all | solution.py:157
  314.3 113.1 %psum.15 = f32[1024]{0:T(1024)S(1)} all-reduce(f32[1024]{0:T(1024)S(1)} %dynamic_update_slice.46), channel_id=1, replica_groups=mesh['ctx'=64,'tp'=8] {'ctx'}, use_global_device_ids=true, to_apply=%region_8.9 | all-reduce | flops 1024 | bytes 8192 | tf_op jit(solution)/shard_map/psum | solution.py:169
  427.9 168.7 %all-reduce.6.cloned.1.call-done = f32[512,128]{1,0:T(8,128)} async-done(((f32[512,128]{1,0:T(8,128)}), f32[512,128]{1,0:T(8,128)}) %all-reduce.6.cloned.1.call-update) | async-done | bytes 262160 | tf_op jit(solution)/shard_map/psum | solution.py:168
  596.7 1.7 broadcast_multiply_fusion
  598.3 1.0 copy.87
  599.3 1.0 copy.88
  600.3 1.0 copy.89
  601.3 1.0 copy.90
  (725 shorter events, 102.9 us)
Async XLA Ops:
  7.2 84.1 %copy-start = (f32[512,128]{1,0:T(8,128)S(1)}, f32[512,128]{1,0:T(8,128)}, u32[]{:S(2)}) copy-start(f32[512,128]{1,0:T(8,128)} %param.13) | copy-start | bytes 786436
  9.3 10.8 %copy-start.2 = (bf16[256,1024]{1,0:T(8,128)(2,1)S(1)}, bf16[256,1024]{1,0:T(8,128)(2,1)}, u32[]{:S(2)}) copy-start(bf16[256,1024]{1,0:T(8,128)(2,1)} %param.11) | copy-start | bytes 1572868
  9.3 25.9 %all-to-all-start.1 = ((bf16[256,64,16]{0,2,1:T(8,128)(2,1)}), bf16[256,64,16]{0,2,1:T(8,128)(2,1)S(1)}, u32[]{:S(2)}, u32[]{:S(2)}) async-start(bf16[256,64,16]{0,2,1:T(8,128)(2,1)} %bitcast.17), calls=%async_computation.1 | async-start | bytes 1048576 | tf_op jit(solution)/shard_map/all_to_all | solution.py:106
  21.1 22.4 %copy-start.3 = (bf16[256,1024]{1,0:T(8,128)(2,1)S(1)}, bf16[256,1024]{1,0:T(8,128)(2,1)}, u32[]{:S(2)}) copy-start(bf16[256,1024]{1,0:T(8,128)(2,1)} %param.9) | copy-start | bytes 1572868
  35.2 23.4 %all-to-all-start.2 = ((bf16[256,64,16]{0,2,1:T(8,128)(2,1)}), bf16[256,64,16]{0,2,1:T(8,128)(2,1)S(1)}, u32[]{:S(2)}, u32[]{:S(2)}) async-start(bf16[256,64,16]{0,2,1:T(8,128)(2,1)} %bitcast.19), calls=%async_computation.2 | async-start | bytes 1048576 | tf_op jit(solution)/shard_map/all_to_all | solution.py:107
  44.5 22.4 %copy-start.4 = (bf16[256,1024]{1,0:T(8,128)(2,1)S(1)}, bf16[256,1024]{1,0:T(8,128)(2,1)}, u32[]{:S(2)}) copy-start(bf16[256,1024]{1,0:T(8,128)(2,1)} %param.12) | copy-start | bytes 1572868
  58.6 23.4 %all-to-all-start = ((bf16[256,64,16]{0,2,1:T(8,128)(2,1)}), bf16[256,64,16]{0,2,1:T(8,128)(2,1)S(1)}, u32[]{:S(2)}, u32[]{:S(2)}) async-start(bf16[256,64,16]{0,2,1:T(8,128)(2,1)} %bitcast.15), calls=%async_computation | async-start | bytes 1048576 | tf_op jit(solution)/shard_map/all_to_all | solution.py:105
  82.0 8.5 %copy-start.8 = (s32[16384]{0:T(1024)S(1)}, s32[16384]{0:T(1024)}, u32[]{:S(2)}) copy-start(s32[16384]{0:T(1024)} %param.15) | copy-start | bytes 196612
  82.0 23.5 %all-to-all-start.3 = ((bf16[256,64,16]{0,2,1:T(8,128)(2,1)}), bf16[256,64,16]{0,2,1:T(8,128)(2,1)S(1)}, u32[]{:S(2)}, u32[]{:S(2)}) async-start(bf16[256,64,16]{0,2,1:T(8,128)(2,1)} %bitcast.21), calls=%async_computation.3 | async-start | bytes 1048576 | tf_op jit(solution)/shard_map/all_to_all | solution.py:108
  234.3 8.4 %copy-start.5 = (bf16[16,1024,16]{1,2,0:T(8,128)(2,1)S(1)}, bf16[16,1024,16]{1,2,0:T(8,128)(2,1)}, u32[]{:S(2)}) copy-start(bf16[16,1024,16]{1,2,0:T(8,128)(2,1)} %get-tuple-element.259) | copy-start | bytes 1572868
  234.3 23.5 %all-to-all-start.4 = ((bf16[64,256,16]{1,2,0:T(8,128)(2,1)}), bf16[64,256,16]{1,2,0:T(8,128)(2,1)S(1)}, u32[]{:S(2)}, u32[]{:S(2)}) async-start(bf16[64,256,16]{1,2,0:T(8,128)(2,1)} %copy.80), calls=%async_computation.4 | async-start | bytes 1048576 | tf_op jit(solution)/shard_map/all_to_all | solution.py:154
  244.5 21.8 %copy-start.6 = (bf16[16,1024,16]{1,2,0:T(8,128)(2,1)S(1)}, bf16[16,1024,16]{1,2,0:T(8,128)(2,1)}, u32[]{:S(2)}) copy-start(bf16[16,1024,16]{1,2,0:T(8,128)(2,1)} %get-tuple-element.260) | copy-start | bytes 1572868
  257.9 23.6 %all-to-all-start.5 = ((bf16[64,256,16]{1,2,0:T(8,128)(2,1)}), bf16[64,256,16]{1,2,0:T(8,128)(2,1)S(1)}, u32[]{:S(2)}, u32[]{:S(2)}) async-start(bf16[64,256,16]{1,2,0:T(8,128)(2,1)} %copy.82), calls=%async_computation.5 | async-start | bytes 1048576 | tf_op jit(solution)/shard_map/all_to_all | solution.py:155
  268.1 21.7 %copy-start.7 = (bf16[16,1024,16]{1,2,0:T(8,128)(2,1)S(1)}, bf16[16,1024,16]{1,2,0:T(8,128)(2,1)}, u32[]{:S(2)}) copy-start(bf16[16,1024,16]{1,2,0:T(8,128)(2,1)} %get-tuple-element.261) | copy-start | bytes 1572868
  281.4 23.4 %all-to-all-start.6 = ((bf16[64,256,16]{1,2,0:T(8,128)(2,1)}), bf16[64,256,16]{1,2,0:T(8,128)(2,1)S(1)}, u32[]{:S(2)}, u32[]{:S(2)}) async-start(bf16[64,256,16]{1,2,0:T(8,128)(2,1)} %copy.84), calls=%async_computation.6 | async-start | bytes 1048576 | tf_op jit(solution)/shard_map/all_to_all | solution.py:156
  304.8 296.5 %all-to-all-start.7 = ((bf16[64,256,16]{1,2,0:T(8,128)(2,1)}), bf16[64,256,16]{1,2,0:T(8,128)(2,1)S(1)}, u32[]{:S(2)}, u32[]{:S(2)}) async-start(bf16[64,256,16]{1,2,0:T(8,128)(2,1)} %copy.86), calls=%async_computation.7 | async-start | bytes 1048576 | tf_op jit(solution)/shard_map/all_to_all | solution.py:157
  313.1 283.6 %all-reduce.6.cloned.1.call-start = ((), (), s32[]{:S(2)}) async-start(), calls=%async_computation.8 | async-start | bytes 524288 | tf_op jit(solution)/shard_map/psum | solution.py:168
  313.2 0.7 copy-start.1
Sparse Core Ops, SparseCore 0:
  319.5 277.1 all-reduce.5
where the time goes:
time: 612 us; the launch traced here: 609 us
  waiting for transfers between devices  265 us (43%)
  blocking collectives  113 us (18%)
  local copies, waits for them, and re-layouts  81.4 us (13%)
  starting transfers between devices  69.2 us (11%)
  other arithmetic  36.6 us (6%)
  matrix products  16.5 us (3%)
  between operations  14.4 us (2%)
  loops' own time  12.7 us (2%)
    psum x1, waiting for transfers between devices, body(): filter_sum = lax.psum(filter_part, ('ctx', 'tp'))  169 us
    psum x1, blocking collectives, body(): bias_sum = lax.psum(bias_part, 'ctx')  113 us
    reduce_sum x16, other arithmetic, hyena_pass(): jnp.sum(signal_grad.astype(jnp.float32) * gated_signal.astype(jnp.float32...  14.1 us
    all_to_all x1, waiting for transfers between devices, body(): lax.all_to_all(queries, 'ctx', split_axis=1, concat_axis=0, tiled=True)  14.1 us
    all_to_all x1, waiting for transfers between devices, body(): lax.all_to_all(key_branch, 'ctx', split_axis=1, concat_axis=0, tiled=True)  14.1 us
    all_to_all x1, waiting for transfers between devices, body(): lax.all_to_all(value_branch, 'ctx', split_axis=1, concat_axis=0, tiled=True)  14.1 us
    all_to_all x1, waiting for transfers between devices, body(): lax.all_to_all(cotangent, 'ctx', split_axis=1, concat_axis=0, tiled=True)  14.1 us
    all_to_all x1, waiting for transfers between devices, body(): lax.all_to_all(results[2], 'ctx', split_axis=0, concat_axis=1, tiled=True)  13.4 us
  transfers between devices with their start and end apart: 9, of which 8 were waited for; matrix products, arithmetic and copies ran while one was open for 2% of the time, Pallas kernels for 0%

commit v1 on v0

--- a/solution.py
+++ b/solution.py
@@ -165,7 +165,7 @@
         pieces[5].sum(axis=0),
         (shard_index * column_count,),
     )
-    filter_sum = lax.psum(filter_part, ("ctx", "tp"))
+    filter_sum = lax.psum(lax.psum(filter_part, "ctx"), "tp")
     bias_sum = lax.psum(bias_part, "ctx")
     grad_filter = filter_sum * (1.0 / math.sqrt(token_count * per_group))
     grad_bias = bias_sum * (1.0 / math.sqrt(token_count))

time: 612 us -> 651 us (1.064)
  the two profiles are of different devices: /device:TPU:23 before, /device:TPU:64 now
where the time goes in v1:
time: 651 us; the launch traced here: 648 us
  waiting for transfers between devices  309 us (47%)
  blocking collectives  126 us (19%)
  local copies, waits for them, and re-layouts  81.4 us (13%)
  starting transfers between devices  51.5 us (8%)
  other arithmetic  36.6 us (6%)
  matrix products  16.5 us (3%)
  between operations  14.4 us (2%)
  loops' own time  12.7 us (2%)
    psum x2, waiting for transfers between devices, body(): filter_sum = lax.psum(lax.psum(filter_part, 'ctx'), 'tp')  195 us
    psum x1, blocking collectives, body(): bias_sum = lax.psum(bias_part, 'ctx')  126 us
    all_to_all x1, waiting for transfers between devices, body(): lax.all_to_all(queries, 'ctx', split_axis=1, concat_axis=0, tiled=True)  16.6 us
    all_to_all x1, waiting for transfers between devices, body(): lax.all_to_all(key_branch, 'ctx', split_axis=1, concat_axis=0, tiled=True)  16.6 us
    all_to_all x1, waiting for transfers between devices, body(): lax.all_to_all(value_branch, 'ctx', split_axis=1, concat_axis=0, tiled=True)  16.6 us
    all_to_all x1, waiting for transfers between devices, body(): lax.all_to_all(cotangent, 'ctx', split_axis=1, concat_axis=0, tiled=True)  16.6 us
    all_to_all x1, waiting for transfers between devices, body(): lax.all_to_all(results[2], 'ctx', split_axis=0, concat_axis=1, tiled=True)  15.9 us
    all_to_all x1, waiting for transfers between devices, body(): lax.all_to_all(results[0], 'ctx', split_axis=0, concat_axis=1, tiled=True)  15.9 us
  transfers between devices with their start and end apart: 10, of which 8 were waited for; matrix products, arithmetic and copies ran while one was open for 2% of the time, Pallas kernels for 0%

profile of v1, /device:TPU:64, one launch (start us, length us, event | category | flops | bytes accessed | tf_op | source)
XLA Modules:
  0.0 648.3 jit_solution(7044058434741038006)
XLA Ops:
  7.2 2.1 copy.73
  9.3 10.7 %all-to-all-start.1 = ((bf16[256,64,16]{0,2,1:T(8,128)(2,1)}), bf16[256,64,16]{0,2,1:T(8,128)(2,1)S(1)}, u32[]{:S(2)}, u32[]{:S(2)}) async-start(bf16[256,64,16]{0,2,1:T(8,128)(2,1)} %bitcast.17), calls=%async_computation.1 | async-start | bytes 1048576 | tf_op jit(solution)/shard_map/all_to_all | solution.py:106
  20.0 1.0 copy.75
  21.0 16.6 %all-to-all-done.1 = bf16[256,64,16]{0,2,1:T(8,128)(2,1)S(1)} async-done(((bf16[256,64,16]{0,2,1:T(8,128)(2,1)}), bf16[256,64,16]{0,2,1:T(8,128)(2,1)S(1)}, u32[]{:S(2)}, u32[]{:S(2)}) %all-to-all-start.1) | async-done | bytes 524320 | tf_op jit(solution)/shard_map/all_to_all | solution.py:106
  37.6 5.8 all-to-all-start.2
  43.4 1.0 copy.71
  44.4 16.6 %all-to-all-done.2 = bf16[256,64,16]{0,2,1:T(8,128)(2,1)S(1)} async-done(((bf16[256,64,16]{0,2,1:T(8,128)(2,1)}), bf16[256,64,16]{0,2,1:T(8,128)(2,1)S(1)}, u32[]{:S(2)}, u32[]{:S(2)}) %all-to-all-start.2) | async-done | bytes 524320 | tf_op jit(solution)/shard_map/all_to_all | solution.py:107
  61.0 5.8 all-to-all-start
  66.8 1.0 copy.77
  67.8 16.6 %all-to-all-done = bf16[256,64,16]{0,2,1:T(8,128)(2,1)S(1)} async-done(((bf16[256,64,16]{0,2,1:T(8,128)(2,1)}), bf16[256,64,16]{0,2,1:T(8,128)(2,1)S(1)}, u32[]{:S(2)}, u32[]{:S(2)}) %all-to-all-start) | async-done | bytes 524320 | tf_op jit(solution)/shard_map/all_to_all | solution.py:105
  84.4 5.9 all-to-all-start.3
  91.3 16.6 %all-to-all-done.3 = bf16[256,64,16]{0,2,1:T(8,128)(2,1)S(1)} async-done(((bf16[256,64,16]{0,2,1:T(8,128)(2,1)}), bf16[256,64,16]{0,2,1:T(8,128)(2,1)S(1)}, u32[]{:S(2)}, u32[]{:S(2)}) %all-to-all-start.3) | async-done | bytes 524320 | tf_op jit(solution)/shard_map/all_to_all | solution.py:108
  108.1 1.0 concatenate.42
  109.1 0.9 multiply_convert_fusion.4
  110.0 1.9 concatenate.44
  111.9 122.1 %while.22 = (s32[]{:T(128)}, bf16[16,1024,16]{1,2,0:T(8,128)(2,1)}, bf16[16,1024,16]{1,2,0:T(8,128)(2,1)}, bf16[16,1024,16]{1,2,0:T(8,128)(2,1)}, bf16[16,1024,1...) while((s32[]{:T(128)}, bf16[16,1024,16]{1,2,0:T(8,128)(2,1)}, ...), condition=%wide.region_4.5_spmd, body=%wide.region_0.4_spmd.sunk | while | flops 28791580 | bytes 4254939 | solution.py:151
  113.9 0.9 fusion.48
  121.6 0.9 fusion.48
  129.2 0.9 fusion.48
  136.8 0.9 fusion.48
  144.5 0.9 fusion.48
  152.1 0.9 fusion.48
  159.7 0.9 fusion.48
  167.4 0.9 fusion.48
  182.6 0.9 fusion.48
  190.3 0.9 fusion.48
  197.9 0.9 fusion.48
  205.5 0.9 fusion.48
  228.4 0.9 fusion.48
  234.0 1.3 copy.79
  235.7 1.1 copy.80
  236.7 5.9 all-to-all-start.4
  243.3 1.1 copy.82
  244.4 15.9 %all-to-all-done.4 = bf16[64,256,16]{1,2,0:T(8,128)(2,1)S(1)} async-done(((bf16[64,256,16]{1,2,0:T(8,128)(2,1)}), bf16[64,256,16]{1,2,0:T(8,128)(2,1)S(1)}, u32[]{:S(2)}, u32[]{:S(2)}) %all-to-all-start.4) | async-done | bytes 524320 | tf_op jit(solution)/shard_map/all_to_all | solution.py:154
  260.3 5.9 all-to-all-start.5
  266.8 1.1 copy.84
  267.9 15.9 %all-to-all-done.5 = bf16[64,256,16]{1,2,0:T(8,128)(2,1)S(1)} async-done(((bf16[64,256,16]{1,2,0:T(8,128)(2,1)}), bf16[64,256,16]{1,2,0:T(8,128)(2,1)S(1)}, u32[]{:S(2)}, u32[]{:S(2)}) %all-to-all-start.5) | async-done | bytes 524320 | tf_op jit(solution)/shard_map/all_to_all | solution.py:155
  283.8 5.8 all-to-all-start.6
  290.2 1.1 copy.86
  291.3 15.9 %all-to-all-done.6 = bf16[64,256,16]{1,2,0:T(8,128)(2,1)S(1)} async-done(((bf16[64,256,16]{1,2,0:T(8,128)(2,1)}), bf16[64,256,16]{1,2,0:T(8,128)(2,1)S(1)}, u32[]{:S(2)}, u32[]{:S(2)}) %all-to-all-start.6) | async-done | bytes 524320 | tf_op jit(solution)/shard_map/all_to_all | solution.py:156
  307.2 5.8 all-to-all-start.7
  313.9 194.9 %all-reduce.7.cloned.1.call-done = f32[512,128]{1,0:T(8,128)} async-done(((f32[512,128]{1,0:T(8,128)}), f32[512,128]{1,0:T(8,128)}) %all-reduce.7.cloned.1.call-update) | async-done | bytes 262160 | tf_op jit(solution)/shard_map/psum | solution.py:168
  509.1 126.0 %psum.23 = f32[1024]{0:T(1024)S(1)} all-reduce(f32[1024]{0:T(1024)S(1)} %dynamic_update_slice.46), channel_id=1, replica_groups=mesh['ctx'=64,'tp'=8] {'ctx'}, use_global_device_ids=true, to_apply=%region_9.10 | all-reduce | flops 1024 | bytes 8192 | tf_op jit(solution)/shard_map/psum | solution.py:169
  635.8 1.7 broadcast_multiply_fusion
  637.4 1.0 copy.87
  638.5 1.0 copy.88
  639.5 1.0 copy.89
  640.5 1.0 copy.90
  (728 shorter events, 103.0 us)
Async XLA Ops:
  7.2 84.0 %copy-start = (f32[512,128]{1,0:T(8,128)S(1)}, f32[512,128]{1,0:T(8,128)}, u32[]{:S(2)}) copy-start(f32[512,128]{1,0:T(8,128)} %param.13) | copy-start | bytes 786436
  9.3 10.7 %copy-start.2 = (bf16[256,1024]{1,0:T(8,128)(2,1)S(1)}, bf16[256,1024]{1,0:T(8,128)(2,1)}, u32[]{:S(2)}) copy-start(bf16[256,1024]{1,0:T(8,128)(2,1)} %param.11) | copy-start | bytes 1572868
  9.3 28.3 %all-to-all-start.1 = ((bf16[256,64,16]{0,2,1:T(8,128)(2,1)}), bf16[256,64,16]{0,2,1:T(8,128)(2,1)S(1)}, u32[]{:S(2)}, u32[]{:S(2)}) async-start(bf16[256,64,16]{0,2,1:T(8,128)(2,1)} %bitcast.17), calls=%async_computation.1 | async-start | bytes 1048576 | tf_op jit(solution)/shard_map/all_to_all | solution.py:106
  21.0 22.4 %copy-start.3 = (bf16[256,1024]{1,0:T(8,128)(2,1)S(1)}, bf16[256,1024]{1,0:T(8,128)(2,1)}, u32[]{:S(2)}) copy-start(bf16[256,1024]{1,0:T(8,128)(2,1)} %param.9) | copy-start | bytes 1572868
  37.6 23.4 %all-to-all-start.2 = ((bf16[256,64,16]{0,2,1:T(8,128)(2,1)}), bf16[256,64,16]{0,2,1:T(8,128)(2,1)S(1)}, u32[]{:S(2)}, u32[]{:S(2)}) async-start(bf16[256,64,16]{0,2,1:T(8,128)(2,1)} %bitcast.19), calls=%async_computation.2 | async-start | bytes 1048576 | tf_op jit(solution)/shard_map/all_to_all | solution.py:107
  44.4 22.4 %copy-start.4 = (bf16[256,1024]{1,0:T(8,128)(2,1)S(1)}, bf16[256,1024]{1,0:T(8,128)(2,1)}, u32[]{:S(2)}) copy-start(bf16[256,1024]{1,0:T(8,128)(2,1)} %param.12) | copy-start | bytes 1572868
  61.0 23.4 %all-to-all-start = ((bf16[256,64,16]{0,2,1:T(8,128)(2,1)}), bf16[256,64,16]{0,2,1:T(8,128)(2,1)S(1)}, u32[]{:S(2)}, u32[]{:S(2)}) async-start(bf16[256,64,16]{0,2,1:T(8,128)(2,1)} %bitcast.15), calls=%async_computation | async-start | bytes 1048576 | tf_op jit(solution)/shard_map/all_to_all | solution.py:105
  84.4 6.0 copy-start.8
  84.4 23.5 %all-to-all-start.3 = ((bf16[256,64,16]{0,2,1:T(8,128)(2,1)}), bf16[256,64,16]{0,2,1:T(8,128)(2,1)S(1)}, u32[]{:S(2)}, u32[]{:S(2)}) async-start(bf16[256,64,16]{0,2,1:T(8,128)(2,1)} %bitcast.21), calls=%async_computation.3 | async-start | bytes 1048576 | tf_op jit(solution)/shard_map/all_to_all | solution.py:108
  236.7 5.9 copy-start.5
  236.7 23.5 %all-to-all-start.4 = ((bf16[64,256,16]{1,2,0:T(8,128)(2,1)}), bf16[64,256,16]{1,2,0:T(8,128)(2,1)S(1)}, u32[]{:S(2)}, u32[]{:S(2)}) async-start(bf16[64,256,16]{1,2,0:T(8,128)(2,1)} %copy.80), calls=%async_computation.4 | async-start | bytes 1048576 | tf_op jit(solution)/shard_map/all_to_all | solution.py:154
  244.4 21.8 %copy-start.6 = (bf16[16,1024,16]{1,2,0:T(8,128)(2,1)S(1)}, bf16[16,1024,16]{1,2,0:T(8,128)(2,1)}, u32[]{:S(2)}) copy-start(bf16[16,1024,16]{1,2,0:T(8,128)(2,1)} %get-tuple-element.260) | copy-start | bytes 1572868
  260.3 23.6 %all-to-all-start.5 = ((bf16[64,256,16]{1,2,0:T(8,128)(2,1)}), bf16[64,256,16]{1,2,0:T(8,128)(2,1)S(1)}, u32[]{:S(2)}, u32[]{:S(2)}) async-start(bf16[64,256,16]{1,2,0:T(8,128)(2,1)} %copy.82), calls=%async_computation.5 | async-start | bytes 1048576 | tf_op jit(solution)/shard_map/all_to_all | solution.py:155
  267.9 21.7 %copy-start.7 = (bf16[16,1024,16]{1,2,0:T(8,128)(2,1)S(1)}, bf16[16,1024,16]{1,2,0:T(8,128)(2,1)}, u32[]{:S(2)}) copy-start(bf16[16,1024,16]{1,2,0:T(8,128)(2,1)} %get-tuple-element.261) | copy-start | bytes 1572868
  283.8 23.4 %all-to-all-start.6 = ((bf16[64,256,16]{1,2,0:T(8,128)(2,1)}), bf16[64,256,16]{1,2,0:T(8,128)(2,1)S(1)}, u32[]{:S(2)}, u32[]{:S(2)}) async-start(bf16[64,256,16]{1,2,0:T(8,128)(2,1)} %copy.84), calls=%async_computation.6 | async-start | bytes 1048576 | tf_op jit(solution)/shard_map/all_to_all | solution.py:156
  307.2 333.2 %all-to-all-start.7 = ((bf16[64,256,16]{1,2,0:T(8,128)(2,1)}), bf16[64,256,16]{1,2,0:T(8,128)(2,1)S(1)}, u32[]{:S(2)}, u32[]{:S(2)}) async-start(bf16[64,256,16]{1,2,0:T(8,128)(2,1)} %copy.86), calls=%async_computation.7 | async-start | bytes 1048576 | tf_op jit(solution)/shard_map/all_to_all | solution.py:157
  313.0 195.8 %all-reduce.7.cloned.1.call-start = ((), (), s32[]{:S(2)}) async-start(), calls=%async_computation.8 | async-start | bytes 524288 | tf_op jit(solution)/shard_map/psum | solution.py:168
  313.1 0.7 copy-start.1
  313.9 321.9 %all-reduce.9.cloned.1.call-start = ((), (), s32[]{:S(2)}) async-start(), calls=%async_computation.9 | async-start | bytes 524288 | tf_op jit(solution)/shard_map/psum | solution.py:168
Sparse Core Ops, SparseCore 0:
  317.8 190.9 all-reduce.6
  511.1 77.8 all-reduce.8
